TPU v7x, 256 devices: a whole 4x4x8 slice. The times are simulated.
256 devices in a mesh: path: 64 (over x, z_lo, y, core), shard: 4 (over z_hi).
Axes of the slice: x: 4, y: 4, z: 8 (z_hi: 4, z_lo: 2; z = z_hi * 2 + z_lo), core: 2. Of those that a mesh axis runs over, the one named last changes fastest.
Arguments:
- path_delta: float32 [64, 2, 512, 1024], P('path', None, 'shard'), may hold values from -500 to 500
- assign: int32 [64, 2], replicated, may hold values from 0 to 15
- params: float32 [32, 4, 128, 1024], P(None, 'shard', 'path'), may hold values from -6 to 6
- momentum: float32 [32, 4, 128, 1024], P(None, 'shard', 'path'), may hold values from -3 to 3
Outputs:
- path_params: float32 [64, 2, 512, 1024], P('path', None, 'shard')
- new_params: float32 [32, 4, 128, 1024], P(None, 'shard', 'path')
- new_momentum: float32 [32, 4, 128, 1024], P(None, 'shard', 'path')
All inputs are finite; a program needn't handle non-finite values.
Results may differ from a plain program's by a relative error of at most 0.00007.
Values sent between devices are 32-bit elements; how exact they have to be, the bound alone decides.
A program may use at most 128 MiB of HBM per device.

v0:
```python
import jax
import jax.numpy as jnp
from jax import lax
from jax.sharding import PartitionSpec as P

LEVEL_MODULES = 16
LEVELS = 2


outer_rate = 0.7
beta_coef = 0.9


def local(path_delta, assign, params, momentum):
    own_slab = path_delta[0]
    path_count = assign.shape[0]
    module_count = params.shape[0]
    own_rows = params.shape[2]
    width = own_slab.shape[2]
    squares = jnp.sum(own_slab * own_slab)
    total_sq = lax.psum(squares, "shard")
    entries = own_slab.shape[0] * own_slab.shape[1] * width * lax.axis_size("shard")
    rescale = 1.0 / jnp.sqrt(total_sq / entries + 1e-06)
    scaled = own_slab * rescale
    offsets = jnp.arange(LEVELS, dtype=jnp.int32) * LEVEL_MODULES
    module_id = assign + offsets[None, :]
    flat_ids = module_id.reshape(-1)
    membership = (flat_ids[:, None] == jnp.arange(module_count, dtype=jnp.int32)[None, :]).astype(
        jnp.float32
    )
    sharers = jnp.sum(membership, axis=0)
    path_here = lax.axis_index("path")
    own_members = lax.dynamic_slice_in_dim(membership, path_here * LEVELS, LEVELS, 0)
    summed = lax.psum_scatter(
        jnp.einsum("lm,lrd->rmd", own_members, scaled, precision=lax.Precision.HIGHEST),
        "path",
        scatter_dimension=0,
        tiled=True,
    )
    summed = jnp.transpose(summed, (1, 0, 2))
    outer_grad = summed / jnp.maximum(sharers, 1.0)[:, None, None]
    new_moment = beta_coef * momentum[:, 0] + outer_grad
    new_state = params[:, 0] - outer_rate * (outer_grad + beta_coef * new_moment)
    outgoing = jnp.take(new_state, flat_ids, axis=0).reshape(path_count, LEVELS, own_rows, width)
    returned = lax.all_to_all(outgoing, "path", split_axis=0, concat_axis=2, tiled=True)[0]
    return (returned[None], new_state[:, None], new_moment[:, None])


def solution(mesh):
    in_specs = (
        P("path", None, "shard", None),
        P(),
        P(None, "shard", "path", None),
        P(None, "shard", "path", None),
    )
    out_specs = (
        P("path", None, "shard", None),
        P(None, "shard", "path", None),
        P(None, "shard", "path", None),
    )
    return jax.shard_map(local, mesh=mesh, in_specs=in_specs, out_specs=out_specs, check_vma=False)
```

profile of v0, /device:TPU:1, one launch (start us, length us, event | category | flops | bytes accessed | tf_op | source)
XLA Modules:
  0.0 392.5 jit_solution(4304714066258396081)
XLA Ops:
  7.2 0.0 reduce-scatter.2.cloned.1.call-start
  7.2 2.1 multiply_reduce_fusion
  9.3 14.3 %psum.7 = f32[]{:T(128)} all-reduce(f32[]{:T(128)} %multiply_reduce_fusion), channel_id=1, replica_groups=mesh['path'=64,'shard'=4] {'shard'}, use_global_device_ids=true, to_apply=%region_1.0 | all-reduce | flops 1 | bytes 8 | tf_op jit(solution)/shard_map/psum | solution.py:21
  24.4 0.8 compare_and_fusion
  25.1 0.1 copy.18
  25.2 0.1 reshape.61
  25.3 0.1 iota_compare_fusion
  25.4 1.3 multiply_bitcast_fusion
  26.7 0.0 copy-start
  26.8 0.0 copy-start.1
  26.8 13.1 %convolution_bitcast_fusion = f32[128,32,1024]{2,1,0:T(8,128)} fusion(f32[2,128,1024]{2,1,0:T(8,128)S(1)} %multiply_bitcast_fusion, pred[128,32]{1,0:T(8,128)(4,1)S(1)} %iota_compare_fusion, s32[]{:T(128)S(6)} %select_n.26), kind=kOutput, calls=%fused_computation.1 | convolution fusion | flops 100663296 | bytes 17826308 | tf_op jit(solution)/shard_map/lm,lrd->rmd/dot_general | solution.py:35
  39.9 0.0 reduce-scatter.2.cloned.1.call-update
  39.9 0.1 reshape.62
  40.1 0.1 copy.16
  40.2 0.1 convert_reduce_fusion
  40.3 310.7 %reduce-scatter.2.cloned.1.call-done = f32[2,32,1024]{2,1,0:T(8,128)} async-done(((f32[128,32,1024]{2,1,0:T(8,128)}), f32[2,32,1024]{2,1,0:T(8,128)}) %reduce-scatter.2.cloned.1.call-update) | async-done | bytes 262160 | tf_op jit(solution)/shard_map/reduce_scatter | solution.py:34
  351.0 0.0 copy-done
  351.0 0.0 copy-done.1
  351.0 1.2 fusion.3
  352.2 0.2 copy.22
  352.4 1.7 gather_fusion
  354.1 1.5 broadcast_select_fusion
  355.6 10.3 %all-to-all-start = ((f32[64,2,2,1024]{3,2,1,0:T(2,128)}), f32[64,2,2,1024]{3,2,1,0:T(2,128)S(1)}, u32[]{:S(2)}, u32[]{:S(2)}) async-start(f32[64,2,2,1024]{3,2,1,0:T(2,128)} %broadcast_select_fusion), calls=%async_computation.1 | async-start | bytes 2097152 | tf_op jit(solution)/shard_map/all_to_all | solution.py:45
  365.9 0.9 copy.25
  366.8 0.9 copy.24
  367.7 16.2 %all-to-all-done = f32[64,2,2,1024]{3,2,1,0:T(2,128)S(1)} async-done(((f32[64,2,2,1024]{3,2,1,0:T(2,128)}), f32[64,2,2,1024]{3,2,1,0:T(2,128)S(1)}, u32[]{:S(2)}, u32[]{:S(2)}) %all-to-all-start) | async-done | bytes 1048608 | tf_op jit(solution)/shard_map/all_to_all | solution.py:45
  383.9 0.1 copy.23
  384.0 1.7 all_to_all.16
  (4 shorter events, 0.0 us)
Async XLA Ops:
  7.2 343.8 %reduce-scatter.2.cloned.1.call-start = ((), (), s32[]{:S(2)}) async-start(), calls=%async_computation.2 | async-start | bytes 17039360 | tf_op jit(solution)/shard_map/reduce_scatter | solution.py:34
  26.7 324.2 %copy-start = (f32[32,1,2,1024]{3,2,1,0:T(2,128)S(1)}, f32[32,1,2,1024]{3,2,1,0:T(2,128)}, u32[]{:S(2)}) copy-start(f32[32,1,2,1024]{3,2,1,0:T(2,128)} %param.7) | copy-start | bytes 786436
  26.8 324.2 %copy-start.1 = (f32[32,1,2,1024]{3,2,1,0:T(2,128)S(1)}, f32[32,1,2,1024]{3,2,1,0:T(2,128)}, u32[]{:S(2)}) copy-start(f32[32,1,2,1024]{3,2,1,0:T(2,128)} %param.6) | copy-start | bytes 786436
  355.6 28.3 %all-to-all-start = ((f32[64,2,2,1024]{3,2,1,0:T(2,128)}), f32[64,2,2,1024]{3,2,1,0:T(2,128)S(1)}, u32[]{:S(2)}, u32[]{:S(2)}) async-start(f32[64,2,2,1024]{3,2,1,0:T(2,128)} %broadcast_select_fusion), calls=%async_computation.1 | async-start | bytes 2097152 | tf_op jit(solution)/shard_map/all_to_all | solution.py:45
Sparse Core Ops, SparseCore 0:
  40.0 310.8 reduce-scatter.1
where the time goes:
time: 393 us
  waiting for transfers between devices  327 us (83%)
  between operations  14.8 us (4%)
  blocking collectives  14.3 us (4%)
  matrix products  13.1 us (3%)
  starting transfers between devices  10.3 us (3%)
  other arithmetic  7.04 us (2%)
  local copies, waits for them, and re-layouts  5.96 us (2%)
    reduce_scatter x1, waiting for transfers between devices, local(): lax.psum_scatter(jnp.einsum('lm,lrd->rmd', own_members, scaled, precision...  311 us
    all_to_all x1, waiting for transfers between devices, local(): lax.all_to_all(outgoing, 'path', split_axis=0, concat_axis=2, tiled=True)[0]  16.2 us
    psum x1, blocking collectives, local(): total_sq = lax.psum(squares, 'shard')  14.3 us
    dot_general x1, matrix products, local(): jnp.einsum('lm,lrd->rmd', own_members, scaled, precision=lax.Precision.HI...  13.1 us
    all_to_all x1, starting transfers between devices, local(): lax.all_to_all(outgoing, 'path', split_axis=0, concat_axis=2, tiled=True)[0]  10.3 us
  transfers between devices with their start and end apart: 2, of which 2 were waited for; matrix products, arithmetic and copies ran while one was open for 1% of the time, Pallas kernels for 0%

commit v1 on v0

v1 whole, which is shorter than its diff:
```python
import jax
import jax.numpy as jnp
from jax import lax
from jax.experimental import pallas as pl
from jax.experimental.pallas import tpu as pltpu
from jax.sharding import PartitionSpec as P

LEVEL_MODULES = 16
LEVELS = 2
PATHS = 64
SHARDS = 4
MODULES = 32
STRIDE = 37

outer_rate = 0.7
beta_coef = 0.9

MESH = pl.DeviceIdType.MESH
f32 = jnp.float32
i32 = jnp.int32


def rem(a, b):
    return lax.rem(a, jnp.int32(b))


def div(a, b):
    return lax.div(a, jnp.int32(b))


def split(p):
    return div(p, 16), rem(div(p, 8), 2), rem(div(p, 2), 4), rem(p, 2)


def step_peers(me, i):
    x, z, y, c = split(me)
    dx, dz, dy, dc = split(rem(i * STRIDE, PATHS))
    to = rem(x + dx, 4) * 16 + rem(z + dz, 2) * 8 + rem(y + dy, 4) * 2 + rem(c + dc, 2)
    frm = rem(x + 4 - dx, 4) * 16 + rem(z + 2 - dz, 2) * 8 + rem(y + 4 - dy, 4) * 2 + rem(c + 2 - dc, 2)
    return to, frm


def kernel(
    x_send, x_sum, assign_ref, par_hbm, mom_hbm,
    ret_ref, newp_hbm, newm_hbm,
    xbuf, par, mom, newp, newm, landed, chain, outgoing,
    own_sq, sq_in, sq_row, sq_shards, itab, ftab, itab_s, ftab_s,
    lsem, sq_send, sq_recv, sh_send, sh_recv, d_send, d_recv, r_send, r_recv, own_sem,
):
    me = lax.axis_index("path")
    shard = lax.axis_index("shard")

    barrier = pltpu.get_barrier_semaphore()

    def greet(i, carry):
        to, _ = step_peers(me, i)
        pl.semaphore_signal(barrier, inc=1, device_id=(to, shard), device_id_type=MESH)
        return carry

    load_x = pltpu.make_async_copy(x_sum, xbuf, lsem.at[0])
    load_p = pltpu.make_async_copy(par_hbm, par, lsem.at[1])
    load_m = pltpu.make_async_copy(mom_hbm, mom, lsem.at[2])
    load_x.start()
    lax.fori_loop(1, PATHS, greet, 0)
    for k in range(1, SHARDS):
        pl.semaphore_signal(barrier, inc=1, device_id=(me, rem(shard + k, SHARDS)), device_id_type=MESH)
    load_p.start()
    load_m.start()

    rows = lax.broadcasted_iota(i32, (PATHS, PATHS), 0)
    lanes = lax.broadcasted_iota(i32, (PATHS, PATHS), 1)
    x, z, y, c = split(me)
    off = (rows * STRIDE) & (PATHS - 1)
    frm = (
        ((x - (off >> 4)) & 3) * 16
        + ((z - ((off >> 3) & 1)) & 1) * 8
        + ((y - ((off >> 1) & 3)) & 3) * 2
        + ((c - (off & 1)) & 1)
    )
    for l in range(LEVELS):
        a_row = assign_ref[l : l + 1, :]
        a_col = jnp.sum(jnp.where(frm == lanes, jnp.broadcast_to(a_row, (PATHS, PATHS)), 0), axis=1, keepdims=True)
        a_mat = jnp.broadcast_to(a_col, (PATHS, PATHS))
        a_by_step = jnp.sum(jnp.where(rows == lanes, a_mat, 0), axis=0, keepdims=True)
        same = (a_mat == jnp.broadcast_to(a_by_step, (PATHS, PATHS))) & (rows < lanes)
        before = jnp.max(jnp.where(same, rows + 1, 0), axis=0, keepdims=True)
        mine = a_mat == lanes
        last = jnp.max(jnp.where(mine, rows + 1, 0), axis=0, keepdims=True)
        count = jnp.sum(jnp.where(mine, 1.0, 0.0).astype(f32), axis=0, keepdims=True)
        itab[l : l + 1, 0:PATHS] = before
        itab[2 + l : 3 + l, 0:PATHS] = last
        itab[4 + l : 5 + l, 0:PATHS] = a_row
        ftab[1 + l : 2 + l, 0:PATHS] = 1.0 / jnp.maximum(count, 1.0)
    ints = pltpu.make_async_copy(itab, itab_s, lsem.at[3])
    ints.start()

    load_x.wait()

    def square(i, acc):
        part = xbuf[pl.ds(i * 16, 16)]
        part = part * part
        return acc + jnp.sum(part.reshape(4, 4, 8, 128), axis=0)

    acc = lax.fori_loop(0, 16, square, jnp.zeros((4, 8, 128), f32))
    total = jnp.sum(acc)
    own_sq[...] = jnp.broadcast_to(total, (1, 128))
    for l in range(LEVELS):
        chain[l, 0] = jnp.zeros((16, 128), f32)

    pl.semaphore_wait(barrier, PATHS - 1 + SHARDS - 1)

    def send_sq(i, carry):
        to, _ = step_peers(me, i)
        pltpu.make_async_remote_copy(
            own_sq, sq_in.at[i - 1], sq_send, sq_recv, device_id=(to, shard), device_id_type=MESH
        ).start()
        return carry

    lax.fori_loop(1, PATHS, send_sq, 0)

    def send_delta(i, carry):
        to, _ = step_peers(me, i)
        pltpu.make_async_remote_copy(
            x_send.at[:, div(to, 4), :, rem(to, 4)], landed.at[i], d_send, d_recv.at[i],
            device_id=(to, shard), device_id_type=MESH,
        ).start()
        return carry

    lax.fori_loop(1, PATHS, send_delta, 0)
    own = pltpu.make_async_copy(x_send.at[:, div(me, 4), :, rem(me, 4)], landed.at[0], own_sem.at[0])
    own.start()

    pltpu.make_async_copy(sq_in, sq_in, sq_recv).wait()
    lane = lax.broadcasted_iota(i32, (1, 128), 1)
    row = jnp.where(lane == 0, own_sq[...], 0.0)
    for i in range(1, PATHS):
        row = row + jnp.where(lane == i, sq_in[i - 1], 0.0)
    sq_row[...] = row
    ints.wait()
    copies = []
    for k in range(1, SHARDS):
        copy = pltpu.make_async_remote_copy(
            sq_row, sq_shards.at[k - 1], sh_send.at[k - 1], sh_recv.at[k - 1],
            device_id=(me, rem(shard + k, SHARDS)), device_id_type=MESH,
        )
        copy.start()
        copies.append(copy)
    for copy in copies:
        copy.wait_recv()
    norm = row + sq_shards[0] + sq_shards[1] + sq_shards[2]
    ftab[0:1, :] = 1.0 / jnp.sqrt(norm / (LEVELS * 512 * 1024) + 1e-06)
    floats = pltpu.make_async_copy(ftab, ftab_s, lsem.at[4])
    floats.start()
    floats.wait()

    arrived = landed.reshape(PATHS, LEVELS, 16, 128)

    def link(i):
        s = ftab_s[0, i]
        for l in range(LEVELS):
            chain[l, i + 1] = arrived[i, l] * s + chain[l, itab_s[l, i]]

    own.wait()
    link(0)

    def add(i, carry):
        pltpu.make_async_copy(landed.at[i], landed.at[i], d_recv.at[i]).wait()
        link(i)
        return carry

    lax.fori_loop(1, PATHS, add, 0)

    load_p.wait()
    load_m.wait()
    for l in range(LEVELS):
        def update(m, carry, l=l):
            grad = chain[l, itab_s[2 + l, m]] * ftab_s[1 + l, m]
            k = l * LEVEL_MODULES + m
            moment = beta_coef * mom[k] + grad
            newm[k] = moment
            newp[k] = par[k] - outer_rate * (grad + beta_coef * moment)
            return carry

        lax.fori_loop(0, LEVEL_MODULES, update, 0, unroll=4)
    put_p = pltpu.make_async_copy(newp, newp_hbm, lsem.at[5])
    put_m = pltpu.make_async_copy(newm, newm_hbm, lsem.at[6])
    put_p.start()
    put_m.start()

    out_view = outgoing.reshape(PATHS, LEVELS, 16, 128)

    def pick(i, carry):
        to, _ = step_peers(me, i)
        for l in range(LEVELS):
            out_view[i, l] = newp[l * LEVEL_MODULES + itab_s[4 + l, to]]
        return carry

    lax.fori_loop(0, PATHS, pick, 0, unroll=4)

    def send_back(i, carry):
        to, _ = step_peers(me, i)
        pltpu.make_async_remote_copy(
            outgoing.at[i], ret_ref.at[:, div(me, 4), :, rem(me, 4)], r_send, r_recv,
            device_id=(to, shard), device_id_type=MESH,
        ).start()
        return carry

    lax.fori_loop(1, PATHS, send_back, 0)
    keep = pltpu.make_async_copy(outgoing.at[0], ret_ref.at[:, div(me, 4), :, rem(me, 4)], own_sem.at[1])
    keep.start()

    for copy in copies:
        copy.wait_send()
    pltpu.make_async_copy(sq_in, sq_in, sq_send).wait()
    rest = outgoing.at[pl.ds(1, PATHS - 1)]
    pltpu.make_async_copy(rest, rest, d_send).wait()
    keep.wait()
    put_p.wait()
    put_m.wait()
    pltpu.make_async_copy(rest, rest, r_send).wait()
    pltpu.make_async_copy(rest, rest, r_recv).wait()


def local(path_delta, assign, params, momentum):
    x_sum = path_delta[0].reshape(2, 16, 8, 8, 128).transpose(0, 1, 3, 2, 4)
    x_send = x_sum.reshape(2, 16, 8, 4, 2, 128)
    x_sum = x_sum.reshape(256, 8, 128)

    def rows_of(a):
        return a.reshape(MODULES, 2, 8, 128).transpose(0, 2, 1, 3).reshape(MODULES, 16, 128)

    def back(a):
        return a.reshape(MODULES, 8, 2, 128).transpose(0, 2, 1, 3).reshape(MODULES, 1, 2, 1024)

    any_space = pl.BlockSpec(memory_space=pl.ANY)
    vm = pltpu.VMEM
    slab = (MODULES, 16, 128)
    dma = pltpu.SemaphoreType.DMA
    ret, newp, newm = pl.pallas_call(
        kernel,
        out_shape=(
            jax.ShapeDtypeStruct((2, 16, 8, 4, 2, 128), f32),
            jax.ShapeDtypeStruct(slab, f32),
            jax.ShapeDtypeStruct(slab, f32),
        ),
        in_specs=[any_space, any_space, pl.BlockSpec(memory_space=pltpu.VMEM), any_space, any_space],
        out_specs=(any_space, any_space, any_space),
        scratch_shapes=[
            vm((256, 8, 128), f32), vm(slab, f32), vm(slab, f32), vm(slab, f32), vm(slab, f32),
            vm((PATHS, LEVELS, 8, 2, 128), f32), vm((LEVELS, PATHS + 1, 16, 128), f32),
            vm((PATHS, LEVELS, 8, 2, 128), f32),
            vm((1, 128), f32), vm((PATHS - 1, 1, 128), f32), vm((1, 128), f32), vm((SHARDS - 1, 1, 128), f32),
            vm((8, 128), i32), vm((8, 128), f32), pltpu.SMEM((8, 128), i32), pltpu.SMEM((8, 128), f32),
            dma((7,)), dma, dma, dma((SHARDS - 1,)), dma((SHARDS - 1,)), dma, dma((PATHS,)), dma, dma, dma((2,)),
        ],
        compiler_params=pltpu.CompilerParams(
            collective_id=1, has_side_effects=True, vmem_limit_bytes=32 * 2**20
        ),
        name="outer_step",
    )(x_send, x_sum, assign.T, rows_of(params[:, 0]), rows_of(momentum[:, 0]))
    path_params = ret.reshape(2, 16, 8, 8, 128).transpose(0, 1, 3, 2, 4).reshape(1, 2, 128, 1024)
    return path_params, back(newp), back(newm)


def solution(mesh):
    in_specs = (
        P("path", None, "shard", None),
        P(),
        P(None, "shard", "path", None),
        P(None, "shard", "path", None),
    )
    out_specs = (
        P("path", None, "shard", None),
        P(None, "shard", "path", None),
        P(None, "shard", "path", None),
    )
    return jax.shard_map(local, mesh=mesh, in_specs=in_specs, out_specs=out_specs, check_vma=False)
```

time: 393 us -> 54 us (0.14)
  waiting for transfers between devices: 327 us -> 0 us
  Pallas kernels: 0 us -> 46.9 us
  blocking collectives: 14.3 us -> 0 us
  between operations: 14.8 us -> 0.65 us
  matrix products: 13.1 us -> 0 us
  starting transfers between devices: 10.3 us -> 0 us
  other arithmetic: 7.04 us -> 0 us
    reduce_scatter x1 -> x0, waiting for transfers between devices: 311 us -> none  [local(): lax.psum_scatter(jnp.einsum('lm,lrd->rmd', own_members, scaled, precision...]
    pallas_call x0 -> x1, Pallas kernels: none -> 46.9 us  [local(): pl.pallas_call(kernel, out_shape=(jax.ShapeDtypeStruct((2, 16, 8, 4, 2, 1...]
    all_to_all x1 -> x0, waiting for transfers between devices: 16.2 us -> none  [local(): lax.all_to_all(outgoing, 'path', split_axis=0, concat_axis=2, tiled=True)[0]]
    psum x1 -> x0, blocking collectives: 14.3 us -> none  [local(): total_sq = lax.psum(squares, 'shard')]
    dot_general x1 -> x0, matrix products: 13.1 us -> none  [local(): jnp.einsum('lm,lrd->rmd', own_members, scaled, precision=lax.Precision.HI...]
    all_to_all x1 -> x0, starting transfers between devices: 10.3 us -> none  [local(): lax.all_to_all(outgoing, 'path', split_axis=0, concat_axis=2, tiled=True)[0]]
    unnamed x6 -> x11, local copies, waits for them, and re-layouts: 1.82 us -> 6.17 us
  transfers between devices with their start and end apart: 2 -> 0, of which waited for: 2 -> 0; matrix products, arithmetic and copies ran while one was open for 1% -> 0% of each run, Pallas kernels for 0% -> 0%
where the time goes in v1:
time: 54 us; the launch traced here: 53.8 us
  Pallas kernels  46.9 us (87%)
  local copies, waits for them, and re-layouts  6.17 us (11%)
  between operations  0.65 us (1%)
    pallas_call x1, Pallas kernels, local(): pl.pallas_call(kernel, out_shape=(jax.ShapeDtypeStruct((2, 16, 8, 4, 2, 1...  46.9 us
    unnamed x11, local copies, waits for them, and re-layouts  6.17 us

profile of v1, /device:TPU:1, one launch (start us, length us, event | category | flops | bytes accessed | tf_op | source)
XLA Modules:
  0.0 53.8 jit_solution(6679957099818174799)
XLA Ops:
  0.6 0.0 copy-start.3
  0.6 0.7 %copy-done.3 = s32[64,2]{0,1:T(2,128)S(1)} copy-done((s32[64,2]{0,1:T(2,128)S(1)}, s32[64,2]{0,1:T(2,128)}, u32[]{:S(2)}) %copy-start.3) | copy-done | bytes 536
  1.3 0.0 copy-start
  1.3 1.2 %copy-done = f32[1,2,128,1024]{3,2,1,0:T(8,128)S(1)} copy-done((f32[1,2,128,1024]{3,2,1,0:T(8,128)S(1)}, f32[1,2,128,1024]{3,2,1,0:T(8,128)}, u32[]{:S(2)}) %copy-start) | copy-done | bytes 1048600
  2.5 0.0 copy-start.1
  2.5 0.9 %copy-done.1 = f32[32,1,2,1024]{3,2,1,0:T(2,128)S(1)} copy-done((f32[32,1,2,1024]{3,2,1,0:T(2,128)S(1)}, f32[32,1,2,1024]{3,2,1,0:T(2,128)}, u32[]{:S(2)}) %copy-start.1) | copy-done | bytes 262168
  3.5 0.0 copy-start.2
  3.5 0.9 %copy-done.2 = f32[32,1,2,1024]{3,2,1,0:T(2,128)S(1)} copy-done((f32[32,1,2,1024]{3,2,1,0:T(2,128)S(1)}, f32[32,1,2,1024]{3,2,1,0:T(2,128)}, u32[]{:S(2)}) %copy-start.2) | copy-done | bytes 262168
  4.4 46.9 %outer_step.1 = (f32[2,16,8,4,2,128]{5,4,3,2,1,0:T(2,128)S(1)}, f32[32,16,128]{2,1,0:T(8,128)S(1)}, f32[32,16,128]{2,1,0:T(8,128)S(1)}) custom-call(f32[2,16,8,4,2,128]{5,4,3,2,1,0:T(2,128)S(1)} %bitcast.33, f32[256,8,128]{2,1,0:T(8,128)S(1)} %bitcast.34, s32[2,64]{1,0:T(2,128)S(1)} %bitcast.40, f32[32,16,128]{2,1,0:T(8,128)S(1)} %bitcast.36, ...), custom_call_target="tpu_custom_call" | custom-call | tf_op jit(solution)/shard_map/outer_step/pallas_call | solution.py:239
  51.4 1.0 %copy.14 = f32[1,2,128,1024]{3,2,1,0:T(8,128)} copy(f32[1,2,128,1024]{3,2,1,0:T(8,128)S(1)} %bitcast.35) | data formatting | bytes 2097152
  52.4 0.7 %copy.15 = f32[32,1,2,1024]{3,2,1,0:T(2,128)} copy(f32[32,1,2,1024]{3,2,1,0:T(2,128)S(1)} %bitcast.39) | data formatting | bytes 524288
  53.1 0.7 %copy.16 = f32[32,1,2,1024]{3,2,1,0:T(2,128)} copy(f32[32,1,2,1024]{3,2,1,0:T(2,128)S(1)} %bitcast.38) | data formatting | bytes 524288
Async XLA Ops:
  0.6 0.7 %copy-start.3 = (s32[64,2]{0,1:T(2,128)S(1)}, s32[64,2]{0,1:T(2,128)}, u32[]{:S(2)}) copy-start(s32[64,2]{0,1:T(2,128)} %param.5) | copy-start | bytes 1540
  1.3 1.2 %copy-start = (f32[1,2,128,1024]{3,2,1,0:T(8,128)S(1)}, f32[1,2,128,1024]{3,2,1,0:T(8,128)}, u32[]{:S(2)}) copy-start(f32[1,2,128,1024]{3,2,1,0:T(8,128)} %param.4) | copy-start | bytes 3145732
  2.5 0.9 %copy-start.1 = (f32[32,1,2,1024]{3,2,1,0:T(2,128)S(1)}, f32[32,1,2,1024]{3,2,1,0:T(2,128)}, u32[]{:S(2)}) copy-start(f32[32,1,2,1024]{3,2,1,0:T(2,128)} %param.6) | copy-start | bytes 786436
  3.5 0.9 %copy-start.2 = (f32[32,1,2,1024]{3,2,1,0:T(2,128)S(1)}, f32[32,1,2,1024]{3,2,1,0:T(2,128)}, u32[]{:S(2)}) copy-start(f32[32,1,2,1024]{3,2,1,0:T(2,128)} %param.7) | copy-start | bytes 786436

commit v2 on v1

v2 whole, which is shorter than its diff:
```python
import jax
import jax.numpy as jnp
from jax import lax
from jax.experimental import pallas as pl
from jax.experimental.pallas import tpu as pltpu
from jax.sharding import PartitionSpec as P

LEVEL_MODULES = 16
LEVELS = 2
PATHS = 64
SHARDS = 4
MODULES = 32
STRIDE = 37
CHUNKS = 2
EARLY = 63
GROUP = 16

outer_rate = 0.7
beta_coef = 0.9

MESH = pl.DeviceIdType.MESH
f32 = jnp.float32
i32 = jnp.int32
WIDE = 8 // CHUNKS
SUB = 2 * WIDE


def digits(p):
    return p // 16, p // 8 % 2, p // 2 % 4, p % 2


class Peers:
    def __init__(self, me):
        rem, div = lax.rem, lax.div
        x, z, y, c = div(me, 16), rem(div(me, 8), 2), rem(div(me, 2), 4), rem(me, 2)
        self.xs = [rem(x + d, 4) for d in range(4)]
        self.zs = [rem(z + d, 2) for d in range(2)]
        self.cs = [rem(c + d, 2) for d in range(2)]
        ys = [rem(y + d, 4) for d in range(4)]
        self.xz = [[a * 16 + b * 8 for b in self.zs] for a in self.xs]
        self.xz_tile = [[a * 4 + b * 2 for b in self.zs] for a in self.xs]
        self.yc = [[a * 2 + b for b in self.cs] for a in ys]
        self.y_tile = [div(a, 2) for a in ys]
        self.yc_pair = [[rem(a, 2) * 2 + b for b in self.cs] for a in ys]

    def to(self, i):
        dx, dz, dy, dc = digits(i * STRIDE % PATHS)
        return self.xz[dx][dz] + self.yc[dy][dc]

    def place(self, i):
        dx, dz, dy, dc = digits(i * STRIDE % PATHS)
        return self.xz_tile[dx][dz] + self.y_tile[dy], self.yc_pair[dy][dc]


def kernel(
    x_send, x_sum, assign_hbm, par_hbm, mom_hbm,
    ret_ref, newp_ref, newm_ref,
    assign_ref, xbuf, par, mom, newp, newm, landed, chain, outgoing,
    own_sq, sq_in, sq_row, sq_shards, itab, ftab, itab_s, ftab_s,
    lsem, sq_send, sq_recv, sh_send, sh_recv, d_send, d_recv, r_send, r_recv, own_sem,
):
    me = lax.axis_index("path")
    shard = lax.axis_index("shard")
    peers = Peers(me)
    shard_peers = [lax.rem(shard + k, SHARDS) for k in range(SHARDS)]
    steps = range(1, PATHS)

    barrier = pltpu.get_barrier_semaphore()
    for i in steps:
        pl.semaphore_signal(barrier, inc=1, device_id=(peers.to(i), shard), device_id_type=MESH)
    for k in range(1, SHARDS):
        pl.semaphore_signal(barrier, inc=1, device_id=(me, shard_peers[k]), device_id_type=MESH)

    load_x = pltpu.make_async_copy(x_sum, xbuf, lsem.at[0])
    load_a = pltpu.make_async_copy(assign_hbm, assign_ref, lsem.at[3])
    load_p = pltpu.make_async_copy(par_hbm, par, lsem.at[1])
    load_m = pltpu.make_async_copy(mom_hbm, mom, lsem.at[2])
    for copy in (load_x, load_a, load_p, load_m):
        copy.start()

    load_a.wait()
    rows = lax.broadcasted_iota(i32, (PATHS, PATHS), 0)
    lanes = lax.broadcasted_iota(i32, (PATHS, PATHS), 1)
    x, z, y, c = lax.div(me, 16), lax.rem(lax.div(me, 8), 2), lax.rem(lax.div(me, 2), 4), lax.rem(me, 2)
    off = (rows * STRIDE) & (PATHS - 1)
    frm = (
        ((x - (off >> 4)) & 3) * 16
        + ((z - ((off >> 3) & 1)) & 1) * 8
        + ((y - ((off >> 1) & 3)) & 3) * 2
        + ((c - (off & 1)) & 1)
    )
    for l in range(LEVELS):
        a_row = assign_ref[l : l + 1, :]
        a_col = jnp.sum(jnp.where(frm == lanes, jnp.broadcast_to(a_row, (PATHS, PATHS)), 0), axis=1, keepdims=True)
        a_mat = jnp.broadcast_to(a_col, (PATHS, PATHS))
        a_by_step = jnp.sum(jnp.where(rows == lanes, a_mat, 0), axis=0, keepdims=True)
        same = (a_mat == jnp.broadcast_to(a_by_step, (PATHS, PATHS))) & (rows < lanes)
        before = jnp.max(jnp.where(same, rows + 1, 0), axis=0, keepdims=True)
        mine = a_mat == lanes
        last = jnp.max(jnp.where(mine, rows + 1, 0), axis=0, keepdims=True)
        count = jnp.sum(jnp.where(mine, 1.0, 0.0).astype(f32), axis=0, keepdims=True)
        itab[l : l + 1, 0:PATHS] = before
        itab[2 + l : 3 + l, 0:PATHS] = last
        itab[4 + l : 5 + l, 0:PATHS] = a_row
        ftab[1 + l : 2 + l, 0:PATHS] = 1.0 / jnp.maximum(count, 1.0)
    ints = pltpu.make_async_copy(itab, itab_s, lsem.at[3])
    ints.start()

    load_x.wait()

    def square(i, acc):
        part = xbuf[pl.ds(i * 16, 16)]
        part = part * part
        return acc + jnp.sum(part.reshape(4, 4, 8, 128), axis=0)

    acc = lax.fori_loop(0, 16, square, jnp.zeros((4, 8, 128), f32))
    own_sq[...] = jnp.broadcast_to(jnp.sum(acc), (1, 128))
    for h in range(CHUNKS):
        for l in range(LEVELS):
            chain[h, l, 0] = jnp.zeros((SUB, 128), f32)
    ints.wait()

    pl.semaphore_wait(barrier, PATHS - 1 + SHARDS - 1)

    for i in steps:
        pltpu.make_async_remote_copy(
            own_sq, sq_in.at[i - 1], sq_send, sq_recv, device_id=(peers.to(i), shard), device_id_type=MESH
        ).start()

    def send_delta(h, i):
        tile, pair = peers.place(i)
        pltpu.make_async_remote_copy(
            x_send.at[:, tile, pl.ds(h * WIDE, WIDE), pair], landed.at[h, i], d_send, d_recv.at[h, i],
            device_id=(peers.to(i), shard), device_id_type=MESH,
        ).start()

    order = [(h, i) for h in range(CHUNKS) for i in steps]
    for h, i in order[:EARLY]:
        send_delta(h, i)
    tile, pair = peers.place(0)
    own = [
        pltpu.make_async_copy(x_send.at[:, tile, pl.ds(h * WIDE, WIDE), pair], landed.at[h, 0], own_sem.at[h])
        for h in range(CHUNKS)
    ]
    for copy in own:
        copy.start()

    pltpu.make_async_copy(sq_in, sq_in, sq_recv).wait()
    lane = lax.broadcasted_iota(i32, (1, 128), 1)
    part = [jnp.where(lane == 0, own_sq[...], 0.0)] + [jnp.where(lane == i, sq_in[i - 1], 0.0) for i in steps]
    while len(part) > 1:
        part = [a + b for a, b in zip(part[::2], part[1::2])]
    row = part[0]
    sq_row[...] = row
    copies = [
        pltpu.make_async_remote_copy(
            sq_row, sq_shards.at[k - 1], sh_send.at[k - 1], sh_recv.at[k - 1],
            device_id=(me, shard_peers[k]), device_id_type=MESH,
        )
        for k in range(1, SHARDS)
    ]
    for copy in copies:
        copy.start()
    for h, i in order[EARLY:]:
        send_delta(h, i)
    for copy in copies:
        copy.wait_recv()
    norm = row + sq_shards[0] + sq_shards[1] + sq_shards[2]
    ftab[0:1, :] = 1.0 / jnp.sqrt(norm / (LEVELS * 512 * 1024) + 1e-06)
    floats = pltpu.make_async_copy(ftab, ftab_s, lsem.at[4])
    floats.start()
    floats.wait()
    load_p.wait()
    load_m.wait()

    arrived = landed.reshape(CHUNKS, PATHS, LEVELS, SUB, 128)
    out_view = outgoing.reshape(CHUNKS, PATHS, LEVELS, SUB, 128)
    my_tile, my_pair = peers.place(0)

    for h in range(CHUNKS):
        for i in range(PATHS):
            if i == 0:
                own[h].wait()
            else:
                pltpu.make_async_copy(landed.at[h, i], landed.at[h, i], d_recv.at[h, i]).wait()
            s = ftab_s[0, i]
            for l in range(LEVELS):
                chain[h, l, i + 1] = arrived[h, i, l] * s + chain[h, l, itab_s[l, i]]

        cols = pl.ds(h * SUB, SUB)
        for l in range(LEVELS):
            for m in range(LEVEL_MODULES):
                k = l * LEVEL_MODULES + m
                grad = chain[h, l, itab_s[2 + l, m]] * ftab_s[1 + l, m]
                moment = beta_coef * mom[k, cols] + grad
                newm[k, cols] = moment
                newp[k, cols] = par[k, cols] - outer_rate * (grad + beta_coef * moment)

        def pick(i):
            to = peers.to(i)
            for l in range(LEVELS):
                out_view[h, i, l] = newp[l * LEVEL_MODULES + itab_s[4 + l, to], cols]

        def send_back(i):
            dst = ret_ref.at[:, my_tile, pl.ds(h * WIDE, WIDE), my_pair]
            if i == 0:
                pltpu.make_async_copy(outgoing.at[h, i], dst, own_sem.at[CHUNKS + h]).start()
            else:
                pltpu.make_async_remote_copy(
                    outgoing.at[h, i], dst, r_send.at[h], r_recv.at[h],
                    device_id=(peers.to(i), shard), device_id_type=MESH,
                ).start()

        todo = [1 + i for i in range(PATHS - 1)] + [0]
        groups = [todo[g : g + GROUP] for g in range(0, PATHS, GROUP)]
        for g in range(len(groups) + 1):
            for i in groups[g] if g < len(groups) else ():
                pick(i)
            for i in groups[g - 1] if g > 0 else ():
                send_back(i)

    put_p = pltpu.make_async_copy(newp, newp_ref, lsem.at[5])
    put_m = pltpu.make_async_copy(newm, newm_ref, lsem.at[6])
    put_p.start()
    put_m.start()
    for copy in copies:
        copy.wait_send()
    pltpu.make_async_copy(sq_in, sq_in, sq_send).wait()
    for h in range(CHUNKS):
        rest = outgoing.at[h, pl.ds(1, PATHS - 1)]
        pltpu.make_async_copy(rest, rest, d_send).wait()
    put_p.wait()
    put_m.wait()
    for h in range(CHUNKS):
        rest = outgoing.at[h, pl.ds(1, PATHS - 1)]
        pltpu.make_async_copy(outgoing.at[h, 0], outgoing.at[h, 0], own_sem.at[CHUNKS + h]).wait()
        pltpu.make_async_copy(rest, rest, r_send.at[h]).wait()
        pltpu.make_async_copy(rest, rest, r_recv.at[h]).wait()


def finish(a, b, c, a_out, b_out, c_out, sem):
    copies = [pltpu.make_async_copy(s, d, sem.at[k]) for k, (s, d) in enumerate(((a, a_out), (b, b_out), (c, c_out)))]
    for copy in copies:
        copy.start()
    for copy in copies:
        copy.wait()


def local(path_delta, assign, params, momentum):
    x_sum = path_delta[0].reshape(2, 16, 8, 8, 128).transpose(0, 1, 3, 2, 4)
    x_send = x_sum.reshape(2, 16, 8, 4, 2, 128)
    x_sum = x_sum.reshape(256, 8, 128)

    def rows_of(a):
        return a.reshape(MODULES, 2, 8, 128).transpose(0, 2, 1, 3).reshape(MODULES, 16, 128)

    def back(a):
        return a.reshape(MODULES, 8, 2, 128).transpose(0, 2, 1, 3).reshape(MODULES, 1, 2, 1024)

    any_space = pl.BlockSpec(memory_space=pl.ANY)
    vm = pltpu.VMEM
    slab = (MODULES, 16, 128)
    dma = pltpu.SemaphoreType.DMA
    operands = (x_send, x_sum, assign.T, rows_of(params[:, 0]), rows_of(momentum[:, 0]))
    ret, newp, newm = pl.pallas_call(
        kernel,
        out_shape=(
            jax.ShapeDtypeStruct((2, 16, 8, 4, 2, 128), f32),
            jax.ShapeDtypeStruct(slab, f32),
            jax.ShapeDtypeStruct(slab, f32),
        ),
        in_specs=[any_space] * 5,
        out_specs=[any_space] * 3,
        scratch_shapes=[
            vm((LEVELS, PATHS), i32), vm((256, 8, 128), f32), vm(slab, f32), vm(slab, f32), vm(slab, f32), vm(slab, f32),
            vm((CHUNKS, PATHS, LEVELS, WIDE, 2, 128), f32), vm((CHUNKS, LEVELS, PATHS + 1, SUB, 128), f32),
            vm((CHUNKS, PATHS, LEVELS, WIDE, 2, 128), f32),
            vm((1, 128), f32), vm((PATHS - 1, 1, 128), f32), vm((1, 128), f32), vm((SHARDS - 1, 1, 128), f32),
            vm((8, 128), i32), vm((8, 128), f32), pltpu.SMEM((8, 128), i32), pltpu.SMEM((8, 128), f32),
            dma((7,)), dma, dma, dma((SHARDS - 1,)), dma((SHARDS - 1,)), dma, dma((CHUNKS, PATHS)),
            dma((CHUNKS,)), dma((CHUNKS,)), dma((2 * CHUNKS,)),
        ],
        compiler_params=pltpu.CompilerParams(
            collective_id=1, has_side_effects=True, vmem_limit_bytes=32 * 2**20
        ),
        name="outer_step",
    )(*[pltpu.with_memory_space_constraint(v, pltpu.HBM) for v in operands])
    outs = (ret.reshape(2, 16, 8, 8, 128), newp, newm)
    ret, newp, newm = pl.pallas_call(
        finish,
        out_shape=[jax.ShapeDtypeStruct(o.shape, o.dtype) for o in outs],
        in_specs=[any_space] * 3,
        out_specs=[any_space] * 3,
        scratch_shapes=[dma((3,))],
        compiler_params=pltpu.CompilerParams(vmem_limit_bytes=2**20),
        name="finish",
    )(*[pltpu.with_memory_space_constraint(v, pltpu.VMEM) for v in outs])
    path_params = ret.transpose(0, 1, 3, 2, 4).reshape(1, 2, 128, 1024)
    return path_params, back(newp), back(newm)


def solution(mesh):
    in_specs = (
        P("path", None, "shard", None),
        P(),
        P(None, "shard", "path", None),
        P(None, "shard", "path", None),
    )
    out_specs = (
        P("path", None, "shard", None),
        P(None, "shard", "path", None),
        P(None, "shard", "path", None),
    )
    return jax.shard_map(local, mesh=mesh, in_specs=in_specs, out_specs=out_specs, check_vma=False)
```

time: 54 us -> 41.7 us (0.77)
  local copies, waits for them, and re-layouts: 6.17 us -> 0 us
  Pallas kernels: 46.9 us -> 40.9 us
    pallas_call x1, Pallas kernels: 46.9 us -> 39.8 us  [local(): pl.pallas_call(kernel, out_shape=(jax.ShapeDtypeStruct((2, 16, 8, 4, 2, 1...]
    unnamed x11 -> x0, local copies, waits for them, and re-layouts: 6.17 us -> none
    pallas_call x0 -> x1, Pallas kernels: none -> 1.16 us  [local(): pl.pallas_call(finish, out_shape=[jax.ShapeDtypeStruct(o.shape, o.dtype)...]
where the time goes in v2:
time: 41.7 us; the launch traced here: 41.6 us
  Pallas kernels  40.9 us (98%)
  between operations  0.64 us (2%)
    pallas_call x1, Pallas kernels, local(): pl.pallas_call(kernel, out_shape=(jax.ShapeDtypeStruct((2, 16, 8, 4, 2, 1...  39.8 us
    pallas_call x1, Pallas kernels, local(): pl.pallas_call(finish, out_shape=[jax.ShapeDtypeStruct(o.shape, o.dtype)...  1.16 us

profile of v2, /device:TPU:1, one launch (start us, length us, event | category | flops | bytes accessed | tf_op | source)
XLA Modules:
  0.0 41.6 jit_solution(50490048812804484)
XLA Ops:
  0.6 39.8 %outer_step.1 = (f32[2,16,8,4,2,128]{5,4,3,2,1,0:T(2,128)S(1)}, f32[32,16,128]{2,1,0:T(8,128)S(1)}, f32[32,16,128]{2,1,0:T(8,128)S(1)}) custom-call(f32[2,16,8,4,2,128]{5,4,3,2,1,0:T(2,128)} %bitcast.33, f32[256,8,128]{2,1,0:T(8,128)} %bitcast.34, s32[2,64]{1,0:T(2,128)} %bitcast.37, f32[32,16,128]{2,1,0:T(8,128)} %bitcast.35, f32[32,16,128]{2,1,0:T(8,128)} %bitcast.36), custom_call_target="tpu_custom_call" | custom-call | tf_op jit(solution)/shard_map/outer_step/pallas_call | solution.py:265
  40.4 1.2 %finish.1 = (f32[2,16,8,8,128]{4,3,2,1,0:T(8,128)}, f32[32,16,128]{2,1,0:T(8,128)}, f32[32,16,128]{2,1,0:T(8,128)}) custom-call(f32[2,16,8,8,128]{4,3,2,1,0:T(8,128)S(1)} %bitcast.32, f32[32,16,128]{2,1,0:T(8,128)S(1)} %get-tuple-element.10.b, f32[32,16,128]{2,1,0:T(8,128)S(1)} %get-tuple-element.11.c), custom_call_target="tpu_custom_call" | custom-call | tf_op jit(solution)/shard_map/finish/pallas_call | solution.py:289

commit v3 on v2

--- a/solution.py
+++ b/solution.py
@@ -10,7 +10,6 @@
 PATHS = 64
 SHARDS = 4
 MODULES = 32
-STRIDE = 37
 CHUNKS = 2
 EARLY = 63
 GROUP = 16
@@ -27,6 +26,30 @@
 
 def digits(p):
     return p // 16, p // 8 % 2, p // 2 % 4, p % 2
+
+
+def links(offset):
+    x, z, y, _ = digits(offset)
+    ring = {0: (0, 0), 1: (1, 0), 2: (1, 1), 3: (0, 1)}
+    return (*ring[x], *ring[y], z)
+
+
+def far_first():
+    left, load, order = list(range(1, PATHS)), (0,) * 5, [0]
+
+    def cost(o):
+        total = [a + b for a, b in zip(load, links(o))]
+        return -sum(links(o)), max(total) - min(total), o * 45 % PATHS
+
+    while left:
+        o = min(left, key=cost)
+        left.remove(o)
+        order.append(o)
+        load = tuple(a + b for a, b in zip(load, links(o)))
+    return order
+
+
+OFFSETS = far_first()
 
 
 class Peers:
@@ -44,11 +67,11 @@
         self.yc_pair = [[rem(a, 2) * 2 + b for b in self.cs] for a in ys]
 
     def to(self, i):
-        dx, dz, dy, dc = digits(i * STRIDE % PATHS)
+        dx, dz, dy, dc = digits(OFFSETS[i])
         return self.xz[dx][dz] + self.yc[dy][dc]
 
     def place(self, i):
-        dx, dz, dy, dc = digits(i * STRIDE % PATHS)
+        dx, dz, dy, dc = digits(OFFSETS[i])
         return self.xz_tile[dx][dz] + self.y_tile[dy], self.yc_pair[dy][dc]
 
 
@@ -56,7 +79,7 @@
     x_send, x_sum, assign_hbm, par_hbm, mom_hbm,
     ret_ref, newp_ref, newm_ref,
     assign_ref, xbuf, par, mom, newp, newm, landed, chain, outgoing,
-    own_sq, sq_in, sq_row, sq_shards, itab, ftab, itab_s, ftab_s,
+    own_sq, sq_in, sq_row, sq_shards, itab, ftab, scale, itab_s, ftab_s,
     lsem, sq_send, sq_recv, sh_send, sh_recv, d_send, d_recv, r_send, r_recv, own_sem,
 ):
     me = lax.axis_index("path")
@@ -66,10 +89,12 @@
     steps = range(1, PATHS)
 
     barrier = pltpu.get_barrier_semaphore()
-    for i in steps:
+    for i in steps[:32]:
         pl.semaphore_signal(barrier, inc=1, device_id=(peers.to(i), shard), device_id_type=MESH)
-    for k in range(1, SHARDS):
+    for k in (2, 1, 3):
         pl.semaphore_signal(barrier, inc=1, device_id=(me, shard_peers[k]), device_id_type=MESH)
+    for i in steps[32:]:
+        pl.semaphore_signal(barrier, inc=1, device_id=(peers.to(i), shard), device_id_type=MESH)
 
     load_x = pltpu.make_async_copy(x_sum, xbuf, lsem.at[0])
     load_a = pltpu.make_async_copy(assign_hbm, assign_ref, lsem.at[3])
@@ -82,7 +107,9 @@
     rows = lax.broadcasted_iota(i32, (PATHS, PATHS), 0)
     lanes = lax.broadcasted_iota(i32, (PATHS, PATHS), 1)
     x, z, y, c = lax.div(me, 16), lax.rem(lax.div(me, 8), 2), lax.rem(lax.div(me, 2), 4), lax.rem(me, 2)
-    off = (rows * STRIDE) & (PATHS - 1)
+    off = jnp.zeros((PATHS, PATHS), i32)
+    for i in range(1, PATHS):
+        off = jnp.where(rows == i, OFFSETS[i], off)
     frm = (
         ((x - (off >> 4)) & 3) * 16
         + ((z - ((off >> 3) & 1)) & 1) * 8
@@ -102,9 +129,11 @@
         itab[l : l + 1, 0:PATHS] = before
         itab[2 + l : 3 + l, 0:PATHS] = last
         itab[4 + l : 5 + l, 0:PATHS] = a_row
-        ftab[1 + l : 2 + l, 0:PATHS] = 1.0 / jnp.maximum(count, 1.0)
+        ftab[l : l + 1, 0:PATHS] = 1.0 / jnp.maximum(count, 1.0)
     ints = pltpu.make_async_copy(itab, itab_s, lsem.at[3])
     ints.start()
+    floats = pltpu.make_async_copy(ftab, ftab_s, lsem.at[4])
+    floats.start()
 
     load_x.wait()
 
@@ -119,6 +148,7 @@
         for l in range(LEVELS):
             chain[h, l, 0] = jnp.zeros((SUB, 128), f32)
     ints.wait()
+    floats.wait()
 
     pl.semaphore_wait(barrier, PATHS - 1 + SHARDS - 1)
 
@@ -166,10 +196,9 @@
     for copy in copies:
         copy.wait_recv()
     norm = row + sq_shards[0] + sq_shards[1] + sq_shards[2]
-    ftab[0:1, :] = 1.0 / jnp.sqrt(norm / (LEVELS * 512 * 1024) + 1e-06)
-    floats = pltpu.make_async_copy(ftab, ftab_s, lsem.at[4])
-    floats.start()
-    floats.wait()
+    rescale = 1.0 / jnp.sqrt(norm / (LEVELS * 512 * 1024) + 1e-06)
+    spread = jnp.where(rows == lanes, jnp.broadcast_to(rescale[:, 0:PATHS], (PATHS, PATHS)), 0.0)
+    scale[...] = jnp.broadcast_to(jnp.sum(spread, axis=1, keepdims=True), (PATHS, 128))
     load_p.wait()
     load_m.wait()
 
@@ -183,7 +212,7 @@
                 own[h].wait()
             else:
                 pltpu.make_async_copy(landed.at[h, i], landed.at[h, i], d_recv.at[h, i]).wait()
-            s = ftab_s[0, i]
+            s = scale[i : i + 1, :]
             for l in range(LEVELS):
                 chain[h, l, i + 1] = arrived[h, i, l] * s + chain[h, l, itab_s[l, i]]
 
@@ -191,7 +220,7 @@
         for l in range(LEVELS):
             for m in range(LEVEL_MODULES):
                 k = l * LEVEL_MODULES + m
-                grad = chain[h, l, itab_s[2 + l, m]] * ftab_s[1 + l, m]
+                grad = chain[h, l, itab_s[2 + l, m]] * ftab_s[l, m]
                 moment = beta_coef * mom[k, cols] + grad
                 newm[k, cols] = moment
                 newp[k, cols] = par[k, cols] - outer_rate * (grad + beta_coef * moment)
@@ -276,7 +305,7 @@
             vm((CHUNKS, PATHS, LEVELS, WIDE, 2, 128), f32), vm((CHUNKS, LEVELS, PATHS + 1, SUB, 128), f32),
             vm((CHUNKS, PATHS, LEVELS, WIDE, 2, 128), f32),
             vm((1, 128), f32), vm((PATHS - 1, 1, 128), f32), vm((1, 128), f32), vm((SHARDS - 1, 1, 128), f32),
-            vm((8, 128), i32), vm((8, 128), f32), pltpu.SMEM((8, 128), i32), pltpu.SMEM((8, 128), f32),
+            vm((8, 128), i32), vm((8, 128), f32), vm((PATHS, 128), f32), pltpu.SMEM((8, 128), i32), pltpu.SMEM((8, 128), f32),
             dma((7,)), dma, dma, dma((SHARDS - 1,)), dma((SHARDS - 1,)), dma, dma((CHUNKS, PATHS)),
             dma((CHUNKS,)), dma((CHUNKS,)), dma((2 * CHUNKS,)),
         ],

time: 41.7 us -> 40 us (0.959)
  Pallas kernels: 40.9 us -> 39.3 us
    pallas_call x1, Pallas kernels: 39.8 us -> 38.1 us  [local(): pl.pallas_call(kernel, out_shape=(jax.ShapeDtypeStruct((2, 16, 8, 4, 2, 1...]
where the time goes in v3:
time: 40 us; the launch traced here: 39.9 us
  Pallas kernels  39.3 us (98%)
  between operations  0.64 us (2%)
    pallas_call x1, Pallas kernels, local(): pl.pallas_call(kernel, out_shape=(jax.ShapeDtypeStruct((2, 16, 8, 4, 2, 1...  38.1 us
    pallas_call x1, Pallas kernels, local(): pl.pallas_call(finish, out_shape=[jax.ShapeDtypeStruct(o.shape, o.dtype)...  1.16 us

profile of v3, /device:TPU:1, one launch (start us, length us, event | category | flops | bytes accessed | tf_op | source)
XLA Modules:
  0.0 39.9 jit_solution(8696322644684772161)
XLA Ops:
  0.6 38.1 %outer_step.1 = (f32[2,16,8,4,2,128]{5,4,3,2,1,0:T(2,128)S(1)}, f32[32,16,128]{2,1,0:T(8,128)S(1)}, f32[32,16,128]{2,1,0:T(8,128)S(1)}) custom-call(f32[2,16,8,4,2,128]{5,4,3,2,1,0:T(2,128)} %bitcast.33, f32[256,8,128]{2,1,0:T(8,128)} %bitcast.34, s32[2,64]{1,0:T(2,128)} %bitcast.37, f32[32,16,128]{2,1,0:T(8,128)} %bitcast.35, f32[32,16,128]{2,1,0:T(8,128)} %bitcast.36), custom_call_target="tpu_custom_call" | custom-call | tf_op jit(solution)/shard_map/outer_step/pallas_call | solution.py:294
  38.8 1.2 %finish.1 = (f32[2,16,8,8,128]{4,3,2,1,0:T(8,128)}, f32[32,16,128]{2,1,0:T(8,128)}, f32[32,16,128]{2,1,0:T(8,128)}) custom-call(f32[2,16,8,8,128]{4,3,2,1,0:T(8,128)S(1)} %bitcast.32, f32[32,16,128]{2,1,0:T(8,128)S(1)} %get-tuple-element.10.b, f32[32,16,128]{2,1,0:T(8,128)S(1)} %get-tuple-element.11.c), custom_call_target="tpu_custom_call" | custom-call | tf_op jit(solution)/shard_map/finish/pallas_call | solution.py:318

commit v4 on v3

--- a/solution.py
+++ b/solution.py
@@ -20,6 +20,7 @@
 MESH = pl.DeviceIdType.MESH
 f32 = jnp.float32
 i32 = jnp.int32
+FIRST = (1,)
 WIDE = 8 // CHUNKS
 SUB = 2 * WIDE
 
@@ -78,7 +79,7 @@
 def kernel(
     x_send, x_sum, assign_hbm, par_hbm, mom_hbm,
     ret_ref, newp_ref, newm_ref,
-    assign_ref, xbuf, par, mom, newp, newm, landed, chain, outgoing,
+    assign_ref, xbuf, par, mom, newp, newm, landed, chain, outgoing, ahead,
     own_sq, sq_in, sq_row, sq_shards, itab, ftab, scale, itab_s, ftab_s,
     lsem, sq_send, sq_recv, sh_send, sh_recv, d_send, d_recv, r_send, r_recv, own_sem,
 ):
@@ -203,6 +204,7 @@
     load_m.wait()
 
     arrived = landed.reshape(CHUNKS, PATHS, LEVELS, SUB, 128)
+    ahead_view = ahead.reshape(len(FIRST), LEVELS, SUB, 128)
     out_view = outgoing.reshape(CHUNKS, PATHS, LEVELS, SUB, 128)
     my_tile, my_pair = peers.place(0)
 
@@ -235,14 +237,38 @@
             if i == 0:
                 pltpu.make_async_copy(outgoing.at[h, i], dst, own_sem.at[CHUNKS + h]).start()
             else:
-                pltpu.make_async_remote_copy(
-                    outgoing.at[h, i], dst, r_send.at[h], r_recv.at[h],
-                    device_id=(peers.to(i), shard), device_id_type=MESH,
-                ).start()
+                to = peers.to(i)
+                copy = pltpu.make_async_remote_copy(
+                    outgoing.at[h, i], dst, r_send.at[h], r_recv.at[h], device_id=(to, shard), device_id_type=MESH
+                )
+                if h < CHUNKS - 1:
+                    copy.start()
+                else:
+                    other = to != FIRST[0]
+                    for p in FIRST[1:]:
+                        other = jnp.logical_and(other, to != p)
+                    pl.when(other)(copy.start)
+
+        def pick_first():
+            for n, p in enumerate(FIRST):
+                for l in range(LEVELS):
+                    ahead_view[n, l] = newp[l * LEVEL_MODULES + itab_s[4 + l, p], cols]
+
+        def send_first():
+            dst = ret_ref.at[:, my_tile, pl.ds(h * WIDE, WIDE), my_pair]
+            for n, p in enumerate(FIRST):
+                copy = pltpu.make_async_remote_copy(
+                    ahead.at[n], dst, r_send.at[h], r_recv.at[h], device_id=(p, shard), device_id_type=MESH
+                )
+                pl.when(me != p)(copy.start)
 
         todo = [1 + i for i in range(PATHS - 1)] + [0]
         groups = [todo[g : g + GROUP] for g in range(0, PATHS, GROUP)]
+        if h == CHUNKS - 1:
+            pick_first()
         for g in range(len(groups) + 1):
+            if g == 1 and h == CHUNKS - 1:
+                send_first()
             for i in groups[g] if g < len(groups) else ():
                 pick(i)
             for i in groups[g - 1] if g > 0 else ():
@@ -303,7 +329,7 @@
         scratch_shapes=[
             vm((LEVELS, PATHS), i32), vm((256, 8, 128), f32), vm(slab, f32), vm(slab, f32), vm(slab, f32), vm(slab, f32),
             vm((CHUNKS, PATHS, LEVELS, WIDE, 2, 128), f32), vm((CHUNKS, LEVELS, PATHS + 1, SUB, 128), f32),
-            vm((CHUNKS, PATHS, LEVELS, WIDE, 2, 128), f32),
+            vm((CHUNKS, PATHS, LEVELS, WIDE, 2, 128), f32), vm((len(FIRST), LEVELS, WIDE, 2, 128), f32),
             vm((1, 128), f32), vm((PATHS - 1, 1, 128), f32), vm((1, 128), f32), vm((SHARDS - 1, 1, 128), f32),
             vm((8, 128), i32), vm((8, 128), f32), vm((PATHS, 128), f32), pltpu.SMEM((8, 128), i32), pltpu.SMEM((8, 128), f32),
             dma((7,)), dma, dma, dma((SHARDS - 1,)), dma((SHARDS - 1,)), dma, dma((CHUNKS, PATHS)),

time: 40 us -> 39.5 us (0.988)
  Pallas kernels: 39.3 us -> 38.8 us
    pallas_call x1, Pallas kernels: 38.1 us -> 37.6 us  [local(): pl.pallas_call(kernel, out_shape=(jax.ShapeDtypeStruct((2, 16, 8, 4, 2, 1...]
where the time goes in v4:
time: 39.5 us; the launch traced here: 39.4 us
  Pallas kernels  38.8 us (98%)
  between operations  0.64 us (2%)
    pallas_call x1, Pallas kernels, local(): pl.pallas_call(kernel, out_shape=(jax.ShapeDtypeStruct((2, 16, 8, 4, 2, 1...  37.6 us
    pallas_call x1, Pallas kernels, local(): pl.pallas_call(finish, out_shape=[jax.ShapeDtypeStruct(o.shape, o.dtype)...  1.16 us

profile of v4, /device:TPU:1, one launch (start us, length us, event | category | flops | bytes accessed | tf_op | source)
XLA Modules:
  0.0 39.4 jit_solution(57052089854897511)
XLA Ops:
  0.6 37.6 %outer_step.1 = (f32[2,16,8,4,2,128]{5,4,3,2,1,0:T(2,128)S(1)}, f32[32,16,128]{2,1,0:T(8,128)S(1)}, f32[32,16,128]{2,1,0:T(8,128)S(1)}) custom-call(f32[2,16,8,4,2,128]{5,4,3,2,1,0:T(2,128)} %bitcast.33, f32[256,8,128]{2,1,0:T(8,128)} %bitcast.34, s32[2,64]{1,0:T(2,128)} %bitcast.37, f32[32,16,128]{2,1,0:T(8,128)} %bitcast.35, f32[32,16,128]{2,1,0:T(8,128)} %bitcast.36), custom_call_target="tpu_custom_call" | custom-call | tf_op jit(solution)/shard_map/outer_step/pallas_call | solution.py:320
  38.2 1.2 %finish.1 = (f32[2,16,8,8,128]{4,3,2,1,0:T(8,128)}, f32[32,16,128]{2,1,0:T(8,128)}, f32[32,16,128]{2,1,0:T(8,128)}) custom-call(f32[2,16,8,8,128]{4,3,2,1,0:T(8,128)S(1)} %bitcast.32, f32[32,16,128]{2,1,0:T(8,128)S(1)} %get-tuple-element.10.b, f32[32,16,128]{2,1,0:T(8,128)S(1)} %get-tuple-element.11.c), custom_call_target="tpu_custom_call" | custom-call | tf_op jit(solution)/shard_map/finish/pallas_call | solution.py:344
